TPU v7x, 256 devices: a whole 4x4x8 slice. The times are simulated.
256 devices in a mesh: rep: 64 (over z, y, core), shard: 4 (over x).
Axes of the slice: x: 4, y: 4, z: 8, core: 2. Of those that a mesh axis runs over, the one named last changes fastest.
Arguments:
- q_grad: float32 [64, 1152, 1152], P('rep', None, 'shard'), may hold values from -16 to 16
- o_grad: float32 [64, 1152, 1152], P('rep', None, 'shard'), may hold values from -16 to 16
- q_error: float32 [64, 1152, 1152], P('rep', None, 'shard'), may hold values from -4 to 4
- o_error: float32 [64, 1152, 1152], P('rep', None, 'shard'), may hold values from -4 to 4
- q_basis: float32 [1152, 32], P('shard'), may hold values from -6 to 6
- o_basis: float32 [1152, 32], P('shard'), may hold values from -6 to 6
- q_moment: float32 [1152, 1152], P('rep', 'shard'), may hold values from -6 to 6
- o_moment: float32 [1152, 1152], P('rep', 'shard'), may hold values from -6 to 6
- q_weight: float32 [1152, 1152], P('rep', 'shard'), may hold values from -0.1875 to 0.1875
- o_weight: float32 [1152, 1152], P('rep', 'shard'), may hold values from -0.1875 to 0.1875
- norm_grads: float32 [64, 4, 2304], P('rep', 'shard'), may hold values from -6 to 6
- norm_moment: float32 [2304], P(('rep', 'shard')), may hold values from -6 to 6
- norm_weight: float32 [2304], P(('rep', 'shard')), may hold values from 0.5 to 1.5
Outputs:
- q_weight_new: float32 [1152, 1152], P(None, 'shard')
- o_weight_new: float32 [1152, 1152], P(None, 'shard')
- q_moment_new: float32 [1152, 1152], P('rep', 'shard')
- o_moment_new: float32 [1152, 1152], P('rep', 'shard')
- q_error_new: float32 [64, 1152, 1152], P('rep', None, 'shard')
- o_error_new: float32 [64, 1152, 1152], P('rep', None, 'shard')
- norm_weight_new: float32 [2304], replicated
- norm_moment_new: float32 [2304], P(('rep', 'shard'))
All inputs are finite; a program needn't handle non-finite values.
Results may differ from a plain program's by a relative error of at most 0.0003.
Values sent between devices are 32-bit elements; how exact they have to be, the bound alone decides.
A program may use at most 64 MiB of HBM per device.

v0:
```python
import jax
import jax.numpy as jnp
from jax import lax
from jax.sharding import PartitionSpec as P

ROUNDS = 2
highest = lax.Precision.HIGHEST
decay_rate = 0.9
step_size = 0.1


def unwhiten(lower, factor):
    return jax.scipy.linalg.solve_triangular(lower, factor.T, lower=True).T


def product(left, right):
    return jnp.dot(left, right, precision=highest)


def per_device(
    q_grad,
    o_grad,
    q_error,
    o_error,
    q_basis,
    o_basis,
    q_moment,
    o_moment,
    q_weight,
    o_weight,
    norm_grads,
    norm_moment,
    norm_weight,
):
    corr_q = q_grad[0] + q_error[0]
    corr_o = o_grad[0] + o_error[0]
    basis_q = q_basis
    basis_o = o_basis
    normal_q = None
    normal_o = None
    for sweep in range(ROUNDS):
        part_q = product(corr_q, basis_q)
        part_o = product(corr_o, basis_o)
        left_q, left_o = lax.psum((part_q, part_o), ("rep", "shard"))
        gram_q = product(left_q.T, left_q)
        gram_o = product(left_o.T, left_o)
        lower_q = jnp.linalg.cholesky(gram_q)
        lower_o = jnp.linalg.cholesky(gram_o)
        normal_q = unwhiten(lower_q, left_q)
        normal_o = unwhiten(lower_o, left_o)
        reduce_q = product(corr_q.T, normal_q)
        reduce_o = product(corr_o.T, normal_o)
        summed_q, summed_o = lax.psum((reduce_q, reduce_o), "rep")
        basis_q = summed_q
        basis_o = summed_o
    decoded_q = product(normal_q, basis_q.T)
    decoded_o = product(normal_o, basis_o.T)
    q_error_new = (corr_q - decoded_q)[None]
    o_error_new = (corr_o - decoded_o)[None]
    row_count = q_moment.shape[0]
    start = lax.axis_index("rep") * row_count
    slice_q = lax.dynamic_slice_in_dim(decoded_q, start, row_count, 0)
    slice_o = lax.dynamic_slice_in_dim(decoded_o, start, row_count, 0)
    q_moment_new = decay_rate * q_moment + slice_q
    o_moment_new = decay_rate * o_moment + slice_o
    weight_q = q_weight - step_size * q_moment_new
    weight_o = o_weight - step_size * o_moment_new
    q_weight_new, o_weight_new = (
        lax.all_gather(weight_q, "rep", axis=0, tiled=True),
        lax.all_gather(weight_o, "rep", axis=0, tiled=True),
    )
    flat_grads = norm_grads.reshape(-1)
    norm_sum = lax.psum_scatter(flat_grads, ("rep", "shard"), scatter_dimension=0, tiled=True)
    norm_moment_new = decay_rate * norm_moment + norm_sum
    gain_share = norm_weight - step_size * norm_moment_new
    norm_weight_new = lax.all_gather(gain_share, ("rep", "shard"), axis=0, tiled=True)
    return (
        q_weight_new,
        o_weight_new,
        q_moment_new,
        o_moment_new,
        q_error_new,
        o_error_new,
        norm_weight_new,
        norm_moment_new,
    )


def solution(mesh):
    return jax.shard_map(
        per_device,
        mesh=mesh,
        in_specs=(
            P("rep", None, "shard"),
            P("rep", None, "shard"),
            P("rep", None, "shard"),
            P("rep", None, "shard"),
            P("shard", None),
            P("shard", None),
            P("rep", "shard"),
            P("rep", "shard"),
            P("rep", "shard"),
            P("rep", "shard"),
            P("rep", "shard", None),
            P(("rep", "shard")),
            P(("rep", "shard")),
        ),
        out_specs=(
            P(None, "shard"),
            P(None, "shard"),
            P("rep", "shard"),
            P("rep", "shard"),
            P("rep", None, "shard"),
            P("rep", None, "shard"),
            P(),
            P(("rep", "shard")),
        ),
        check_vma=False,
    )
```

profile of v0, /device:TPU:1, one launch (start us, length us, event | category | flops | bytes accessed | tf_op | source)
XLA Modules:
  0.0 1079.3 jit_solution(495348832060264353)
XLA Ops:
  7.2 2.0 add.52
  13.3 252.6 %all-reduce.13.cloned.1.call-done = (f32[1152,32]{0,1:T(8,128)}, f32[1152,32]{0,1:T(8,128)}) async-done(((f32[1152,32]{0,1:T(8,128)}, f32[1152,32]{0,1:T(8,128)}), (f32[1152,32]{0,1:T(8,128)}, f32[1152,32]{0,1:T(8,128)})) %all-reduce.13.cloned.1.call-update) | async-done | bytes 294928 | tf_op jit(solution)/shard_map/psum | solution.py:44
  268.5 2.9 cholesky.96
  272.8 2.4 custom-call.10
  276.5 1.8 fusion.4
  278.4 2.9 cholesky.74
  282.7 2.4 custom-call.8
  285.5 1.8 fusion.13
  287.4 169.6 %all-reduce.17.cloned.1.call-done = (f32[288,32]{0,1:T(8,128)}, f32[288,32]{0,1:T(8,128)}) async-done(((f32[288,32]{0,1:T(8,128)}, f32[288,32]{0,1:T(8,128)}), (f32[288,32]{0,1:T(8,128)}, f32[288,32]{0,1:T(8,128)})) %all-reduce.17.cloned.1.call-update) | async-done | bytes 73744 | tf_op jit(solution)/shard_map/psum | solution.py:53
  457.0 2.4 fusion.11
  461.3 247.8 %all-reduce.11.cloned.1.call-done = (f32[1152,32]{0,1:T(8,128)}, f32[1152,32]{0,1:T(8,128)}) async-done(((f32[1152,32]{0,1:T(8,128)}, f32[1152,32]{0,1:T(8,128)}), (f32[1152,32]{0,1:T(8,128)}, f32[1152,32]{0,1:T(8,128)})) %all-reduce.11.cloned.1.call-update) | async-done | bytes 294928 | tf_op jit(solution)/shard_map/psum | solution.py:44
  711.6 2.9 cholesky.107
  715.9 2.4 custom-call.11
  719.7 2.9 cholesky.85
  723.9 2.4 custom-call.9
  727.7 1.8 fusion.9
  729.5 1.8 fusion
  732.6 168.4 %all-reduce.15.cloned.1.call-done = (f32[288,32]{0,1:T(8,128)}, f32[288,32]{0,1:T(8,128)}) async-done(((f32[288,32]{0,1:T(8,128)}, f32[288,32]{0,1:T(8,128)}), (f32[288,32]{0,1:T(8,128)}, f32[288,32]{0,1:T(8,128)})) %all-reduce.15.cloned.1.call-update) | async-done | bytes 73744 | tf_op jit(solution)/shard_map/psum | solution.py:53
  901.0 2.1 fusion.42
  909.8 77.3 %all-reduce.1 = f32[2304]{0:T(1024)S(1)} all-reduce(f32[2304]{0:T(1024)S(1)} %reduce.4), channel_id=2, replica_groups=mesh['rep'=64,'shard'=4] {'rep','shard'}, use_global_device_ids=true, to_apply=%region_10.13.clone | all-reduce | flops 2304 | bytes 18432
  987.8 73.1 %all-reduce = f32[2304]{0:T(1024)} all-reduce(f32[2304]{0:T(1024)S(1)} %get-tuple-element.42), channel_id=1, replica_groups=mesh['rep'=64,'shard'=4] {'rep','shard'}, use_global_device_ids=true, to_apply=%add | all-reduce | flops 2304 | bytes 18432
  1062.3 3.5 fusion.8
  1065.8 1.7 reshape.35
  1069.1 1.7 reshape.33
  (95 shorter events, 33.8 us)
Async XLA Ops:
  7.2 2.0 copy-start
  7.2 258.7 %all-reduce.13.cloned.1.call-start = ((), (), s32[]{:S(2)}) async-start(), calls=%async_computation.3 | async-start | bytes 589824 | tf_op jit(solution)/shard_map/psum | solution.py:44
  7.2 3.6 copy-start.5
  9.2 1.6 copy-start.4
  10.8 0.8 copy-start.7
  13.2 443.8 %all-reduce.17.cloned.1.call-start = ((), (), s32[]{:S(2)}) async-start(), calls=%async_computation.5 | async-start | bytes 196608 | tf_op jit(solution)/shard_map/psum | solution.py:53
  265.9 19.2 %copy-start.3 = (f32[1152,32]{0,1:T(8,128)S(1)}, f32[1152,32]{0,1:T(8,128)}, u32[]{:S(2)}) copy-start(f32[1152,32]{0,1:T(8,128)} %get-tuple-element.36) | copy-start | bytes 442372
  287.4 421.7 %all-reduce.11.cloned.1.call-start = ((), (), s32[]{:S(2)}) async-start(), calls=%async_computation.2 | async-start | bytes 589824 | tf_op jit(solution)/shard_map/psum | solution.py:44
  457.0 2.4 copy-start.9
  461.0 440.0 %all-reduce.15.cloned.1.call-start = ((), (), s32[]{:S(2)}) async-start(), calls=%async_computation.4 | async-start | bytes 196608 | tf_op jit(solution)/shard_map/psum | solution.py:53
  727.6 3.8 copy-start.10
  727.7 3.9 copy-start.11
  729.5 2.2 copy-start.12
  729.5 2.3 copy-start.13
  731.4 334.4 %all-gather.7.cloned.1.call-start = ((), (), s32[]{:S(2)}) async-start(), calls=%async_computation.1 | async-start | bytes 2396160 | tf_op jit(solution)/shard_map/all_gather | solution.py:70
  901.0 2.1 copy-start.8
  901.0 4.4 copy-start.6
  903.1 3.2 copy-start.1
  904.4 1.1 copy-start.2
  905.5 4.3 copy-start.14
  905.5 81.7 %copy-start.15 = (f32[9]{0:T(128)S(1)}, f32[9]{0:T(128)}, u32[]{:S(2)}) copy-start(f32[9]{0:T(128)} %param.28) | copy-start | bytes 112
  905.5 81.7 %copy-start.16 = (f32[9]{0:T(128)S(1)}, f32[9]{0:T(128)}, u32[]{:S(2)}) copy-start(f32[9]{0:T(128)} %param.27) | copy-start | bytes 112
  908.0 161.1 %all-gather.5.cloned.1.call-start = ((), (), s32[]{:S(2)}) async-start(), calls=%async_computation | async-start | bytes 2396160 | tf_op jit(solution)/shard_map/all_gather | solution.py:69
Sparse Core Ops, SparseCore 0:
  14.2 251.6 all-reduce.12
  287.5 169.5 all-reduce.16
  463.2 245.7 all-reduce.10
  731.5 169.4 all-reduce.14
  908.1 75.9 all-gather.6
  986.6 75.1 all-gather.4
where the time goes:
time: 1080 us
  waiting for transfers between devices  839 us (78%)
  blocking collectives  150 us (14%)
  other arithmetic  33.9 us (3%)
  matrix products  27.1 us (3%)
  local copies, waits for them, and re-layouts  14.5 us (1%)
  between operations  14.4 us (1%)
    psum x2, waiting for transfers between devices, per_device(): left_q, left_o = lax.psum((part_q, part_o), ('rep', 'shard'))  500 us
    psum x2, waiting for transfers between devices, per_device(): summed_q, summed_o = lax.psum((reduce_q, reduce_o), 'rep')  338 us
    unnamed x2, blocking collectives  150 us
    dot_general x14, matrix products, product(): return jnp.dot(left, right, precision=highest)  22.9 us
  transfers between devices with their start and end apart: 6, of which 4 were waited for; matrix products, arithmetic and copies ran while one was open for 1% of the time, Pallas kernels for 0%

commit v1 on v0

--- a/solution.py
+++ b/solution.py
@@ -2,6 +2,7 @@
 import jax.numpy as jnp
 from jax import lax
 from jax.sharding import PartitionSpec as P
+from jax.lax import psum
 
 ROUNDS = 2
 highest = lax.Precision.HIGHEST
@@ -41,7 +42,13 @@
     for sweep in range(ROUNDS):
         part_q = product(corr_q, basis_q)
         part_o = product(corr_o, basis_o)
-        left_q, left_o = lax.psum((part_q, part_o), ("rep", "shard"))
+
+        def _start_patches(base_x):
+            for m in ("shard", "rep"):
+                base_x = psum(base_x, axis_name=m)
+            return base_x
+
+        left_q, left_o = _start_patches((part_q, part_o))
         gram_q = product(left_q.T, left_q)
         gram_o = product(left_o.T, left_o)
         lower_q = jnp.linalg.cholesky(gram_q)

time: 1080 us -> 1040 us (0.963)
  waiting for transfers between devices: 839 us -> 802 us
    psum x2 -> x4, waiting for transfers between devices: 500 us -> 461 us  [_start_patches(): base_x = psum(base_x, axis_name=m)]
  transfers between devices with their start and end apart: 6 -> 8, of which waited for: 4 -> 6; matrix products, arithmetic and copies ran while one was open for 1% -> 1% of each run, Pallas kernels for 0% -> 0%
where the time goes in v1:
time: 1040 us
  waiting for transfers between devices  802 us (77%)
  blocking collectives  151 us (15%)
  other arithmetic  33.9 us (3%)
  matrix products  27.1 us (3%)
  local copies, waits for them, and re-layouts  14.5 us (1%)
  between operations  14.5 us (1%)
    psum x4, waiting for transfers between devices, _start_patches(): base_x = psum(base_x, axis_name=m)  461 us
    psum x2, waiting for transfers between devices, per_device(): summed_q, summed_o = lax.psum((reduce_q, reduce_o), 'rep')  341 us
    unnamed x2, blocking collectives  151 us
    dot_general x14, matrix products, product(): return jnp.dot(left, right, precision=highest)  22.9 us
  transfers between devices with their start and end apart: 8, of which 6 were waited for; matrix products, arithmetic and copies ran while one was open for 1% of the time, Pallas kernels for 0%

profile of v1, /device:TPU:1, one launch (start us, length us, event | category | flops | bytes accessed | tf_op | source)
XLA Modules:
  0.0 1042.8 jit_solution(5659803415435870185)
XLA Ops:
  7.2 2.0 add.60
  13.3 48.9 %all-reduce.25.cloned.1.call-done = (f32[1152,32]{0,1:T(8,128)}, f32[1152,32]{0,1:T(8,128)}) async-done(((f32[1152,32]{0,1:T(8,128)}, f32[1152,32]{0,1:T(8,128)}), (f32[1152,32]{0,1:T(8,128)}, f32[1152,32]{0,1:T(8,128)})) %all-reduce.25.cloned.1.call-update) | async-done | bytes 294928 | tf_op jit(solution)/shard_map/psum | solution.py:48
  62.2 184.8 %all-reduce.21.cloned.1.call-done = (f32[1152,32]{0,1:T(8,128)}, f32[1152,32]{0,1:T(8,128)}) async-done(((f32[1152,32]{0,1:T(8,128)}, f32[1152,32]{0,1:T(8,128)}), (f32[1152,32]{0,1:T(8,128)}, f32[1152,32]{0,1:T(8,128)})) %all-reduce.21.cloned.1.call-update) | async-done | bytes 294928 | tf_op jit(solution)/shard_map/psum | solution.py:48
  249.7 2.9 cholesky.96
  253.9 2.4 custom-call.10
  257.6 1.8 fusion.4
  259.5 2.9 cholesky.74
  263.8 2.4 custom-call.8
  266.6 1.8 fusion.13
  268.5 170.8 %all-reduce.17.cloned.1.call-done = (f32[288,32]{0,1:T(8,128)}, f32[288,32]{0,1:T(8,128)}) async-done(((f32[288,32]{0,1:T(8,128)}, f32[288,32]{0,1:T(8,128)}), (f32[288,32]{0,1:T(8,128)}, f32[288,32]{0,1:T(8,128)})) %all-reduce.17.cloned.1.call-update) | async-done | bytes 73744 | tf_op jit(solution)/shard_map/psum | solution.py:60
  439.4 2.4 fusion.11
  443.4 43.0 %all-reduce.23.cloned.1.call-done = (f32[1152,32]{0,1:T(8,128)}, f32[1152,32]{0,1:T(8,128)}) async-done(((f32[1152,32]{0,1:T(8,128)}, f32[1152,32]{0,1:T(8,128)}), (f32[1152,32]{0,1:T(8,128)}, f32[1152,32]{0,1:T(8,128)})) %all-reduce.23.cloned.1.call-update) | async-done | bytes 294928 | tf_op jit(solution)/shard_map/psum | solution.py:48
  486.7 184.4 %all-reduce.19.cloned.1.call-done = (f32[1152,32]{0,1:T(8,128)}, f32[1152,32]{0,1:T(8,128)}) async-done(((f32[1152,32]{0,1:T(8,128)}, f32[1152,32]{0,1:T(8,128)}), (f32[1152,32]{0,1:T(8,128)}, f32[1152,32]{0,1:T(8,128)})) %all-reduce.19.cloned.1.call-update) | async-done | bytes 294928 | tf_op jit(solution)/shard_map/psum | solution.py:48
  673.7 2.9 cholesky.107
  677.9 2.4 custom-call.11
  681.7 2.9 cholesky.85
  686.0 2.4 custom-call.9
  689.7 1.8 fusion.9
  691.6 1.8 fusion
  694.6 169.8 %all-reduce.15.cloned.1.call-done = (f32[288,32]{0,1:T(8,128)}, f32[288,32]{0,1:T(8,128)}) async-done(((f32[288,32]{0,1:T(8,128)}, f32[288,32]{0,1:T(8,128)}), (f32[288,32]{0,1:T(8,128)}, f32[288,32]{0,1:T(8,128)})) %all-reduce.15.cloned.1.call-update) | async-done | bytes 73744 | tf_op jit(solution)/shard_map/psum | solution.py:60
  864.5 2.1 fusion.42
  873.2 77.3 %all-reduce.1 = f32[2304]{0:T(1024)S(1)} all-reduce(f32[2304]{0:T(1024)S(1)} %reduce.4), channel_id=2, replica_groups=mesh['rep'=64,'shard'=4] {'rep','shard'}, use_global_device_ids=true, to_apply=%region_14.17.clone | all-reduce | flops 2304 | bytes 18432
  951.2 73.2 %all-reduce = f32[2304]{0:T(1024)} all-reduce(f32[2304]{0:T(1024)S(1)} %get-tuple-element.46), channel_id=1, replica_groups=mesh['rep'=64,'shard'=4] {'rep','shard'}, use_global_device_ids=true, to_apply=%add | all-reduce | flops 2304 | bytes 18432
  1025.8 3.5 fusion.8
  (101 shorter events, 37.4 us)
Async XLA Ops:
  7.2 2.0 copy-start
  7.2 55.0 %all-reduce.25.cloned.1.call-start = ((), (), s32[]{:S(2)}) async-start(), calls=%async_computation.7 | async-start | bytes 589824 | tf_op jit(solution)/shard_map/psum | solution.py:48
  7.2 3.6 copy-start.5
  9.2 1.6 copy-start.4
  13.2 233.8 %all-reduce.21.cloned.1.call-start = ((), (), s32[]{:S(2)}) async-start(), calls=%async_computation.5 | async-start | bytes 589824 | tf_op jit(solution)/shard_map/psum | solution.py:48
  62.2 377.2 %all-reduce.17.cloned.1.call-start = ((), (), s32[]{:S(2)}) async-start(), calls=%async_computation.3 | async-start | bytes 196608 | tf_op jit(solution)/shard_map/psum | solution.py:60
  247.0 19.2 %copy-start.3 = (f32[1152,32]{0,1:T(8,128)S(1)}, f32[1152,32]{0,1:T(8,128)}, u32[]{:S(2)}) copy-start(f32[1152,32]{0,1:T(8,128)} %get-tuple-element.40) | copy-start | bytes 442372
  268.5 218.0 %all-reduce.23.cloned.1.call-start = ((), (), s32[]{:S(2)}) async-start(), calls=%async_computation.6 | async-start | bytes 589824 | tf_op jit(solution)/shard_map/psum | solution.py:48
  439.4 2.4 copy-start.9
  443.4 227.7 %all-reduce.19.cloned.1.call-start = ((), (), s32[]{:S(2)}) async-start(), calls=%async_computation.4 | async-start | bytes 589824 | tf_op jit(solution)/shard_map/psum | solution.py:48
  486.4 378.0 %all-reduce.15.cloned.1.call-start = ((), (), s32[]{:S(2)}) async-start(), calls=%async_computation.2 | async-start | bytes 196608 | tf_op jit(solution)/shard_map/psum | solution.py:60
  689.7 3.8 copy-start.10
  689.7 3.9 copy-start.11
  691.6 2.2 copy-start.12
  691.6 2.3 copy-start.13
  693.4 335.9 %all-gather.7.cloned.1.call-start = ((), (), s32[]{:S(2)}) async-start(), calls=%async_computation.1 | async-start | bytes 2396160 | tf_op jit(solution)/shard_map/all_gather | solution.py:77
  864.5 2.1 copy-start.8
  864.5 4.4 copy-start.6
  866.5 3.2 copy-start.1
  867.8 1.1 copy-start.2
  868.9 4.3 copy-start.14
  868.9 81.7 %copy-start.15 = (f32[9]{0:T(128)S(1)}, f32[9]{0:T(128)}, u32[]{:S(2)}) copy-start(f32[9]{0:T(128)} %param.28) | copy-start | bytes 112
  868.9 81.7 %copy-start.16 = (f32[9]{0:T(128)S(1)}, f32[9]{0:T(128)}, u32[]{:S(2)}) copy-start(f32[9]{0:T(128)} %param.27) | copy-start | bytes 112
  871.4 161.2 %all-gather.5.cloned.1.call-start = ((), (), s32[]{:S(2)}) async-start(), calls=%async_computation | async-start | bytes 2396160 | tf_op jit(solution)/shard_map/all_gather | solution.py:76
  (1 other events, 0.8 us)
Sparse Core Ops, SparseCore 0:
  13.4 48.7 all-reduce.24
  65.7 181.2 all-reduce.20
  268.6 170.7 all-reduce.16
  443.5 42.8 all-reduce.22
  489.8 181.2 all-reduce.18
  693.6 170.8 all-reduce.14
  871.5 75.9 all-gather.6
  950.2 75.0 all-gather.4
